TPU v7x, 32 devices: a whole 2x2x4 slice. The times are simulated.
32 devices in a mesh: groups: 2 (over y), wide: 4 (over z), narrow: 4 (over x, core).
Axes of the slice: x: 2, y: 2, z: 4, core: 2. Of those that a mesh axis runs over, the one named last changes fastest.
Arguments:
- inputs: bfloat16 [40, 2, 8192], P('groups', None, 'narrow'), parts along dimension 0, may hold values from -6 to 6
- xz_weight: bfloat16 [8192, 2, 16384], P('narrow', None, 'wide'), may hold values from -0.0625 to 0.0625
- bc_weight: bfloat16 [8192, 4096], P('narrow', 'wide'), may hold values from -0.0625 to 0.0625
- dt_weight: bfloat16 [8192, 256], P('narrow', 'wide'), may hold values from -0.0625 to 0.0625
- conv_x_weight: bfloat16 [4, 256, 64], P(None, 'wide', 'narrow'), may hold values from -3 to 3
- conv_x_bias: bfloat16 [256, 64], P('wide', 'narrow'), may hold values from -3 to 3
- conv_bc_weight: bfloat16 [4, 4096], P(None, 'wide'), may hold values from -3 to 3
- conv_bc_bias: bfloat16 [4096], P('wide'), may hold values from -3 to 3
- conv_x_state: bfloat16 [40, 3, 256, 64], P('groups', None, 'wide', 'narrow'), parts along dimension 0, may hold values from -6 to 6
- conv_bc_state: bfloat16 [40, 3, 4096], P('groups', None, 'wide'), parts along dimension 0, may hold values from -6 to 6
- dt_bias: float32 [256], P('wide'), may hold values from -4 to 0
- a_log: float32 [256], P('wide'), may hold values from 0 to 2.5
- d_skip: float32 [256], P('wide'), may hold values from 0.5 to 2
- norm_weight: bfloat16 [256, 64], P('wide', 'narrow'), may hold values from 0.099609375 to 1.8984375
- out_weight: bfloat16 [256, 64, 8192], P(None, 'narrow', 'wide'), may hold values from -0.046875 to 0.046875
- ssm_state: float32 [40, 256, 64, 256], P('groups', 'wide', 'narrow'), parts along dimension 0, may hold values from -4 to 4
Outputs:
- layer_out: bfloat16 [40, 2, 8192], P('groups', None, ('wide', 'narrow')), parts along dimension 0
- new_ssm_state: float32 [40, 256, 64, 256], P('groups', 'wide', 'narrow'), parts along dimension 0
- new_conv_x: bfloat16 [40, 3, 256, 64], P('groups', None, 'wide', 'narrow'), parts along dimension 0
- new_conv_bc: bfloat16 [40, 3, 4096], P('groups', None, 'wide'), parts along dimension 0
There are 2 independent parts, one for each index of `groups`. A program takes and returns all parts, laid end to end along the dimension named above; an argument that names none is the same for every part. Nothing has to cross between parts.
All inputs are finite; a program needn't handle non-finite values.
Results may differ from a plain program's by a relative error of at most 0.015.
Values may be sent and summed in bfloat16 or wider, within the bound.
A program may use at most 192 MiB of HBM per device.

v0:
```python
import jax
import jax.numpy as jnp
from jax import lax
from jax.sharding import PartitionSpec as P

HEADS = 256
HEAD_DIM = 64
STATE = 256
NGROUPS = 8


EPSILON = 1e-05


def shortened(value):

    def short(part):
        return part.astype(jnp.bfloat16) if part.dtype == jnp.float32 else part

    return jax.tree.map(short, value)


def swapped(value, axis, bit):
    mask = 2**bit
    pairs = [(source, source ^ mask) for source in range(lax.axis_size(axis))]
    return lax.ppermute(value, axis, pairs)


def conv_tokens(history, fresh_vals, tap_weights, offset):
    window = jnp.concatenate([history, fresh_vals], axis=1)
    outputs = []
    for token_idx in range(2):
        summed = offset.astype(jnp.float32)
        for tap_idx in range(tap_weights.shape[0]):
            summed = summed + tap_weights[tap_idx].astype(jnp.float32) * window[
                :, token_idx + tap_idx
            ].astype(jnp.float32)
        outputs.append(jax.nn.silu(summed))
    return (jnp.stack(outputs, axis=1), window[:, 2:])


def advance(ssm_now, x_tok, b_tok, c_tok, dt_tok, dt_bias, a_log, d_skip):
    step_size = jax.nn.softplus(dt_tok.astype(jnp.float32) + dt_bias)
    decay_now = jnp.exp(-step_size * jnp.exp(a_log))
    inject = (step_size[:, :, None] * x_tok)[..., None] * b_tok[:, :, None, :]
    ssm_now = decay_now[:, :, None, None] * ssm_now + inject
    readout = jnp.sum(ssm_now * c_tok[:, :, None, :], axis=-1) + d_skip[None, :, None] * x_tok
    return (ssm_now, readout)


def shards(
    inputs,
    xz_weight,
    bc_weight,
    dt_weight,
    conv_x_weight,
    conv_x_bias,
    conv_bc_weight,
    conv_bc_bias,
    conv_x_state,
    conv_bc_state,
    dt_bias,
    a_log,
    d_skip,
    norm_weight,
    out_weight,
    ssm_state,
):
    seq_count = inputs.shape[0]
    row_count = seq_count * 2
    tok_rows = inputs.reshape(row_count, inputs.shape[2])
    head_local = dt_weight.shape[1]
    wide_count = lax.axis_size("wide")
    narrow_count = lax.axis_size("narrow")
    wide_index = lax.axis_index("wide")
    chan_local = HEAD_DIM // narrow_count
    xz_local = xz_weight.reshape(xz_weight.shape[0], 2, head_local, HEAD_DIM)
    bc_part = jnp.dot(tok_rows, bc_weight, preferred_element_type=jnp.float32)
    dt_part = jnp.dot(tok_rows, dt_weight, preferred_element_type=jnp.float32)
    xz_mine = lax.psum_scatter(
        jnp.einsum("rd,dzhc->czrh", tok_rows, xz_local, preferred_element_type=jnp.float32),
        "narrow",
        scatter_dimension=0,
        tiled=True,
    )
    bc_summed, dt_summed = lax.psum((bc_part, dt_part), "narrow")
    xz_mine = xz_mine.astype(jnp.bfloat16)
    xz_mine = jnp.transpose(xz_mine, (1, 2, 3, 0)).reshape(2, seq_count, 2, head_local, chan_local)
    gate_vals = xz_mine[0]
    x_proj = xz_mine[1]
    bc_proj = bc_summed.astype(jnp.bfloat16).reshape(seq_count, 2, bc_summed.shape[1])
    dt_proj = dt_summed.astype(jnp.bfloat16).reshape(seq_count, 2, head_local)
    x_conv, new_conv_x = conv_tokens(conv_x_state, x_proj, conv_x_weight, conv_x_bias)
    bc_conv, new_conv_bc = conv_tokens(conv_bc_state, bc_proj, conv_bc_weight, conv_bc_bias)
    group_local = max(NGROUPS // wide_count, 1)
    group_span = max(wide_count // NGROUPS, 1)
    bc_mine = bc_conv.reshape(row_count, bc_conv.shape[2])
    for bit_idx in range(group_span.bit_length() - 1):
        partner = swapped(shortened(bc_mine), "wide", bit_idx).astype(bc_mine.dtype)
        is_lower = wide_index // (1 << bit_idx) % 2 == 0
        bc_mine = jnp.where(
            is_lower,
            jnp.concatenate([bc_mine, partner], axis=1),
            jnp.concatenate([partner, bc_mine], axis=1),
        )
    bc_heads = bc_mine.reshape(seq_count, 2, group_local, 2, STATE)
    per_group = head_local // group_local
    b_heads = jnp.repeat(bc_heads[:, :, :, 0], per_group, axis=2)
    c_heads = jnp.repeat(bc_heads[:, :, :, 1], per_group, axis=2)
    ssm_now = ssm_state
    readouts = []
    for token_idx in range(2):
        ssm_now, readout = advance(
            ssm_now,
            x_conv[:, token_idx],
            b_heads[:, token_idx],
            c_heads[:, token_idx],
            dt_proj[:, token_idx],
            dt_bias,
            a_log,
            d_skip,
        )
        readouts.append(readout)
    y_all = jnp.stack(readouts, axis=1)
    gated_out = y_all * jax.nn.silu(gate_vals.astype(jnp.float32))
    grouped = gated_out.reshape(seq_count, 2, group_local, per_group * chan_local)
    squares_part = jnp.sum(grouped * grouped, axis=-1)
    group_sum = lax.psum(squares_part, "narrow")
    for bit_idx in range(group_span.bit_length() - 1):
        group_sum = group_sum + swapped(group_sum, "wide", bit_idx)
    inverse = lax.rsqrt(group_sum / (HEADS // NGROUPS * HEAD_DIM) + EPSILON)
    normed = (grouped * inverse[..., None]).reshape(
        seq_count, 2, head_local, chan_local
    ) * norm_weight.astype(jnp.float32)
    normed = normed.astype(jnp.bfloat16).reshape(row_count, head_local, chan_local)
    out_part = jnp.einsum(
        "rhc,hcd->rd",
        lax.all_gather(normed, "wide", axis=1, tiled=True),
        out_weight,
        preferred_element_type=jnp.float32,
    )
    out_mine = lax.psum_scatter(
        out_part.astype(jnp.bfloat16), "narrow", scatter_dimension=1, tiled=True
    )
    layer_out = out_mine.reshape(seq_count, 2, out_mine.shape[1])
    return (layer_out, ssm_now, new_conv_x, new_conv_bc)


def solution(mesh):
    return jax.shard_map(
        shards,
        mesh=mesh,
        in_specs=(
            P("groups", None, "narrow"),
            P("narrow", None, "wide"),
            P("narrow", "wide"),
            P("narrow", "wide"),
            P(None, "wide", "narrow"),
            P("wide", "narrow"),
            P(None, "wide"),
            P("wide"),
            P("groups", None, "wide", "narrow"),
            P("groups", None, "wide"),
            P("wide"),
            P("wide"),
            P("wide"),
            P("wide", "narrow"),
            P(None, "narrow", "wide"),
            P("groups", "wide", "narrow", None),
        ),
        out_specs=(
            P("groups", None, ("wide", "narrow")),
            P("groups", "wide", "narrow", None),
            P("groups", None, "wide", "narrow"),
            P("groups", None, "wide"),
        ),
        check_vma=False,
    )
```

profile of v0, /device:TPU:0, one launch (start us, length us, event | category | flops | bytes accessed | tf_op | source)
XLA Modules:
  0.0 250.9 jit_solution(5239584444995894743)
XLA Ops:
  7.2 80.9 %copy.186 = bf16[2048,2,4096]{0,2,1:T(8,128)(2,1)} copy(bf16[2048,2,4096]{2,1,0:T(2,128)(2,1)} %param.17) | data formatting | bytes 67108864 | tf_op args[1]
  88.3 21.7 %convolution_bitcast_fusion.1 = f32[64,2,40,64]{0,2,3,1:T(8,128)S(1)} fusion(bf16[2048,2,64,64]{0,3,2,1:T(8,128)(2,1)} %bitcast.177, bf16[40,2048,1,1]{1,0,2,3:T(8,128)(2,1)S(1)} %reshape.347), kind=kOutput, calls=%fused_computation.6 | convolution fusion | flops 1342177280 | bytes 35028992 | tf_op jit(solution)/shard_map/rd,dzhc->czrh/dot_general | solution.py:81
  110.0 2.1 copy.187
  112.2 3.0 %fusion.60 = f32[40,1024]{1,0:T(8,128)S(1)} fusion(bf16[40,2048]{1,0:T(8,128)(2,1)S(1)} %reshape.324, bf16[2048,1024]{1,0:T(8,128)(2,1)} %param.18), kind=kOutput, calls=%fused_computation.124 | convolution fusion | flops 167772160 | bytes 4521984 | tf_op jit(solution)/shard_map/dot_general | solution.py:78
  115.2 0.2 fusion.59
  115.5 15.5 %all-reduce.2 = (bf16[40,1024]{1,0:T(8,128)(2,1)S(1)}, bf16[40,64]{1,0:T(8,128)(2,1)S(1)}) all-reduce(f32[40,1024]{1,0:T(8,128)S(1)} %fusion.60, f32[40,64]{1,0:T(8,128)S(1)} %fusion.59), channel_id=1, replica_groups=mesh['groups'=2,'wide'=4,'narrow'=4] {'narrow'}, use_global_device_ids=true, to_apply=%region_2.0 | all-reduce | flops 43520 | bytes 261120 | tf_op jit(solution)/shard_map/psum | solution.py:86
  131.1 0.6 copy-done.9
  131.7 1.0 divide_multiply_fusion
  133.1 0.2 copy.215
  133.3 0.9 copy.214
  134.2 0.7 copy.185
  134.9 0.7 copy.183
  135.6 0.7 copy.181
  136.3 0.7 copy.179
  137.0 1.4 copy.178
  138.4 0.7 exp.82
  139.0 1.3 convert_element_type.253
  140.3 1.3 multiply_exponential_fusion
  141.9 0.2 broadcast_in_dim.5
  142.1 0.3 slice_bitcast_fusion.2
  142.4 0.2 broadcast_in_dim.4
  142.6 1.8 slice_bitcast_fusion.3
  144.4 5.1 %reduce-scatter.3.cloned.1.call-done = f32[16,2,40,64]{3,2,1,0:T(8,128)} async-done(((f32[64,2,40,64]{3,2,1,0:T(8,128)}), f32[16,2,40,64]{3,2,1,0:T(8,128)}) %reduce-scatter.3.cloned.1.call-update) | async-done | bytes 327696 | tf_op jit(solution)/shard_map/reduce_scatter | solution.py:80
  149.5 1.3 copy.234
  150.8 0.7 copy-done.4
  151.5 0.7 copy-done.5
  152.2 0.7 fusion.56
  152.8 1.8 copy.217
  154.6 1.8 copy.218
  156.4 2.0 multiply_multiply_fusion.1
  158.5 21.2 %multiply_reduce_fusion = (f32[20,64,16]{2,1,0:T(8,128)S(1)}, f32[20,64,16,256]{3,2,1,0:T(8,128)}, f32[20,64,16]{2,1,0:T(8,128)S(1)}) fusion(f32[20,64,256]{2,1,0:T(8,128)S(1)} %get-tuple-element.10, f32[20,64,256]{2,1,0:T(8,128)} %get-tuple-element.12, f32[20,64,16]{2,1,0:T(8,128)S(1)} %get-tuple-element.16, f32[20,64,256]{2,1,0:T(8,128)} %get-tuple-element.11, ...), kind=kLoop, calls=%fused_computation | loop fusion | flops 52387840 | bytes 47523840 | tf_op jit(solution)/shard_map/reduce_sum | solution.py:47
  179.7 0.8 bitcast_add_fusion.1
  180.5 0.2 copy.199
  180.7 0.4 stack.30
  181.1 0.2 copy.198
  181.3 0.4 stack.29
  181.8 0.5 stack.32
  182.3 0.4 copy.201
  182.7 1.1 fusion.40
  184.1 5.7 %psum.23 = f32[20,2,2]{0,2,1:T(2,128)S(1)} all-reduce(f32[20,2,2]{0,2,1:T(2,128)S(1)} %copy.204), channel_id=1, replica_groups=mesh['groups'=2,'wide'=4,'narrow'=4] {'narrow'}, use_global_device_ids=true, to_apply=%region_7.8 | all-reduce | flops 80 | bytes 640 | tf_op jit(solution)/shard_map/psum | solution.py:128
  190.2 1.1 fusion.39
  191.3 0.3 copy.206
  191.6 22.6 %all_gather.3 = bf16[40,256,16]{0,2,1:T(8,128)(2,1)S(1)} all-gather(bf16[40,64,16]{0,2,1:T(8,128)(2,1)S(1)} %copy.206), channel_id=1, replica_groups=mesh['groups'=2,'wide'=4,'narrow'=4] {'wide'}, dimensions={1}, use_global_device_ids=true | all-gather | bytes 409600 | tf_op jit(solution)/shard_map/all_gather | solution.py:138
  214.3 9.5 %fusion = bf16[40,2048]{1,0:T(8,128)(2,1)} fusion(bf16[40,256,16]{0,2,1:T(8,128)(2,1)S(1)} %all_gather.3, bf16[256,16,2048]{2,1,0:T(8,128)(2,1)} %param.30), kind=kOutput, calls=%fused_computation.5 | convolution fusion | flops 671170560 | bytes 17268736 | tf_op jit(solution)/shard_map/rhc,hcd->rd/dot_general | solution.py:136
  223.8 0.7 pad_maximum_fusion.3
  224.5 0.7 pad_maximum_fusion.1
  225.3 17.4 %reduce-scatter.5.cloned.1.call-done = bf16[40,512]{1,0:T(8,128)(2,1)} async-done(((bf16[40,2048]{1,0:T(8,128)(2,1)}), bf16[40,512]{1,0:T(8,128)(2,1)}) %reduce-scatter.5.cloned.1.call-update) | async-done | bytes 40976 | tf_op jit(solution)/shard_map/reduce_scatter | solution.py:142
  242.7 1.4 reshape.330
  (72 shorter events, 1.8 us)
Async XLA Ops:
  7.2 108.1 %copy-start = (bf16[2048,64]{0,1:T(8,128)(2,1)S(1)}, bf16[2048,64]{0,1:T(8,128)(2,1)}, u32[]{:S(2)}) copy-start(bf16[2048,64]{0,1:T(8,128)(2,1)} %param.19) | copy-start | bytes 786436
  7.2 81.0 %copy-start.11 = (bf16[20,2,2048]{2,1,0:T(2,128)(2,1)S(1)}, bf16[20,2,2048]{2,1,0:T(2,128)(2,1)}, u32[]{:S(2)}) copy-start(bf16[20,2,2048]{2,1,0:T(2,128)(2,1)} %param.16) | copy-start | bytes 491524
  7.2 142.3 %reduce-scatter.3.cloned.1.call-start = ((), (), s32[]{:S(2)}) async-start(), calls=%async_computation.2 | async-start | bytes 3276800 | tf_op jit(solution)/shard_map/reduce_scatter | solution.py:80
  88.2 42.8 %copy-start.20 = (bf16[1024]{0:T(1024)(128)(2,1)S(1)}, bf16[1024]{0:T(1024)(128)(2,1)}, u32[]{:S(2)}) copy-start(bf16[1024]{0:T(1024)(128)(2,1)} %param.23) | copy-start | bytes 6148
  88.2 42.8 %copy-start.18 = (bf16[4,1024]{1,0:T(4,128)(2,1)S(1)}, bf16[4,1024]{1,0:T(4,128)(2,1)}, u32[]{:S(2)}) copy-start(bf16[4,1024]{1,0:T(4,128)(2,1)} %param.22) | copy-start | bytes 24580
  88.3 44.6 %copy-start.7 = (bf16[20,3,64,16]{2,3,1,0:T(8,128)(2,1)S(1)}, bf16[20,3,64,16]{2,3,1,0:T(8,128)(2,1)}, u32[]{:S(2)}) copy-start(bf16[20,3,64,16]{2,3,1,0:T(8,128)(2,1)} %param.24) | copy-start | bytes 368644
  88.3 45.9 %copy-start.19 = (bf16[4,64,16]{1,2,0:T(8,128)(2,1)S(1)}, bf16[4,64,16]{1,2,0:T(8,128)(2,1)}, u32[]{:S(2)}) copy-start(bf16[4,64,16]{1,2,0:T(8,128)(2,1)} %param.20) | copy-start | bytes 24580
  112.1 130.6 %reduce-scatter.5.cloned.1.call-start = ((), (), s32[]{:S(2)}) async-start(), calls=%async_computation.3 | async-start | bytes 204800 | tf_op jit(solution)/shard_map/reduce_scatter | solution.py:142
  131.0 0.6 copy-start.9
  150.8 0.7 copy-start.4
  151.5 0.7 copy-start.5
  158.4 21.3 %copy-start.1 = (bf16[20,1,64,16]{3,2,0,1:T(8,128)(2,1)S(1)}, bf16[20,1,64,16]{3,2,0,1:T(8,128)(2,1)}, u32[]{:S(2)}) copy-start(bf16[20,1,64,16]{3,2,0,1:T(8,128)(2,1)} %copy.214) | copy-start | bytes 122884
  158.4 21.3 %copy-start.2 = (bf16[20,1,64,16]{3,2,0,1:T(8,128)(2,1)S(1)}, bf16[20,1,64,16]{3,2,0,1:T(8,128)(2,1)}, u32[]{:S(2)}) copy-start(bf16[20,1,64,16]{3,2,0,1:T(8,128)(2,1)} %copy.217) | copy-start | bytes 122884
  158.4 21.3 %copy-start.3 = (bf16[20,1,64,16]{3,2,0,1:T(8,128)(2,1)S(1)}, bf16[20,1,64,16]{3,2,0,1:T(8,128)(2,1)}, u32[]{:S(2)}) copy-start(bf16[20,1,64,16]{3,2,0,1:T(8,128)(2,1)} %copy.218) | copy-start | bytes 122884
  158.4 21.3 %copy-start.13 = (f32[64,16]{1,0:T(8,128)S(1)}, f32[64,16]{1,0:T(8,128)}, u32[]{:S(2)}) copy-start(f32[64,16]{1,0:T(8,128)} %copy.185) | copy-start | bytes 12292
  158.4 21.3 %copy-start.14 = (f32[64,16]{1,0:T(8,128)S(1)}, f32[64,16]{1,0:T(8,128)}, u32[]{:S(2)}) copy-start(f32[64,16]{1,0:T(8,128)} %copy.183) | copy-start | bytes 12292
  158.4 21.3 %copy-start.15 = (f32[64,16]{1,0:T(8,128)S(1)}, f32[64,16]{1,0:T(8,128)}, u32[]{:S(2)}) copy-start(f32[64,16]{1,0:T(8,128)} %copy.181) | copy-start | bytes 12292
  158.5 21.3 %copy-start.16 = (f32[64,16]{1,0:T(8,128)S(1)}, f32[64,16]{1,0:T(8,128)}, u32[]{:S(2)}) copy-start(f32[64,16]{1,0:T(8,128)} %copy.179) | copy-start | bytes 12292
  158.5 21.3 %copy-start.17 = (f32[64,16]{1,0:T(8,128)S(1)}, f32[64,16]{1,0:T(8,128)}, u32[]{:S(2)}) copy-start(f32[64,16]{1,0:T(8,128)} %copy.178) | copy-start | bytes 12292
  158.5 21.3 %copy-start.21 = (f32[64]{0:T(128)S(1)}, f32[64]{0:T(128)}, u32[]{:S(2)}) copy-start(f32[64]{0:T(128)} %param.28) | copy-start | bytes 772
  181.7 42.1 %copy-start.10 = (bf16[20,2,1024]{2,0,1:T(8,128)(2,1)S(1)}, bf16[20,2,1024]{2,0,1:T(8,128)(2,1)}, u32[]{:S(2)}) copy-start(bf16[20,2,1024]{2,0,1:T(8,128)(2,1)} %copy-done.9) | copy-start | bytes 245764
  181.7 42.1 %copy-start.12 = (bf16[20,3,1024]{2,0,1:T(8,128)(2,1)S(1)}, bf16[20,3,1024]{2,0,1:T(8,128)(2,1)}, u32[]{:S(2)}) copy-start(bf16[20,3,1024]{2,0,1:T(8,128)(2,1)} %param.25) | copy-start | bytes 368644
  181.8 42.7 %copy-start.6 = (bf16[1,40,64,16]{2,3,1,0:T(8,128)(2,1)S(1)}, bf16[1,40,64,16]{2,3,1,0:T(8,128)(2,1)}, u32[]{:S(2)}) copy-start(bf16[1,40,64,16]{2,3,1,0:T(8,128)(2,1)} %copy-done.5) | copy-start | bytes 245764
  181.8 42.7 %copy-start.8 = (bf16[20,3,64,16]{2,3,1,0:T(8,128)(2,1)S(1)}, bf16[20,3,64,16]{2,3,1,0:T(8,128)(2,1)}, u32[]{:S(2)}) copy-start(bf16[20,3,64,16]{2,3,1,0:T(8,128)(2,1)} %param.24) | copy-start | bytes 368644
Sparse Core Ops, SparseCore 0:
  112.2 37.1 reduce-scatter.2
  223.9 18.6 reduce-scatter.4
where the time goes:
time: 254 us; the launch traced here: 251 us
  local copies, waits for them, and re-layouts  104 us (41%)
  blocking collectives  43.9 us (17%)
  matrix products  34.4 us (14%)
  other arithmetic  31.4 us (12%)
  waiting for transfers between devices  22.5 us (9%)
  between operations  14.6 us (6%)
    unnamed x52, local copies, waits for them, and re-layouts  87.9 us
    all_gather x1, blocking collectives, shards(): lax.all_gather(normed, 'wide', axis=1, tiled=True)  22.6 us
    dot_general x1, matrix products, shards(): jnp.einsum('rd,dzhc->czrh', tok_rows, xz_local, preferred_element_type=jn...  21.7 us
    reduce_sum x1, other arithmetic, advance(): jnp.sum(ssm_now * c_tok[:, :, None, :], axis=-1)  21.2 us
    reduce_scatter x1, waiting for transfers between devices, shards(): lax.psum_scatter(out_part.astype(jnp.bfloat16), 'narrow', scatter_dimensi...  17.4 us
    psum x1, blocking collectives, shards(): bc_summed, dt_summed = lax.psum((bc_part, dt_part), 'narrow')  15.5 us
    dot_general x1, matrix products, shards(): jnp.einsum('rhc,hcd->rd', lax.all_gather(normed, 'wide', axis=1, tiled=Tr...  9.51 us
    psum x1, blocking collectives, shards(): group_sum = lax.psum(squares_part, 'narrow')  5.73 us
  transfers between devices with their start and end apart: 2, of which 2 were waited for; matrix products, arithmetic and copies ran while one was open for 7% of the time, Pallas kernels for 0%

commit v1 on v0

--- a/solution.py
+++ b/solution.py
@@ -1,6 +1,10 @@
+import functools
+
 import jax
 import jax.numpy as jnp
 from jax import lax
+from jax.experimental import pallas as pl
+from jax.experimental.pallas import tpu as pltpu
 from jax.sharding import PartitionSpec as P
 
 HEADS = 256
@@ -46,6 +50,347 @@
     ssm_now = decay_now[:, :, None, None] * ssm_now + inject
     readout = jnp.sum(ssm_now * c_tok[:, :, None, :], axis=-1) + d_skip[None, :, None] * x_tok
     return (ssm_now, readout)
+
+
+VMEM_BYTES = 60 << 20
+MESH = pl.DeviceIdType.MESH
+F32 = jnp.float32
+BF16 = jnp.bfloat16
+
+
+def shift_of(value):
+    return value.bit_length() - 1
+
+
+def greet(axes):
+    barrier = pltpu.get_barrier_semaphore()
+    total = 0
+    for axis in axes:
+        count = lax.axis_size(axis)
+        me = lax.axis_index(axis)
+        for hop in range(1, count):
+            pl.semaphore_signal(
+                barrier, inc=1, device_id={axis: lax.rem(me + hop, count)}, device_id_type=MESH
+            )
+        total += count - 1
+    pl.semaphore_wait(barrier, total)
+
+
+def project_kernel(
+    slots,
+    x_ref,
+    dt_ref,
+    w_ref,
+    bc_ref,
+    mine_ref,
+    small_ref,
+    ring,
+    bc_buf,
+    wide_x,
+    order,
+    stage,
+    arrived,
+    small_stage,
+    small_arrived,
+    ring_sem,
+    bc_sem,
+    send_sem,
+    recv_sem,
+    small_send,
+    small_recv,
+):
+    parts = lax.axis_size("narrow")
+    me = lax.axis_index("narrow")
+    depth = w_ref.shape[0]
+    span = 128 * parts
+    blocks = w_ref.shape[2] // span
+    rows = x_ref.shape[0]
+    bc_columns = bc_ref.shape[1]
+    dt_columns = dt_ref.shape[0]
+    chan = HEAD_DIM // parts
+
+    def fetches(block, slot):
+        return [
+            pltpu.make_async_copy(
+                w_ref.at[:, :, pl.ds(pl.multiple_of(block * span + piece * 128, 128), 128)],
+                ring.at[slot, piece],
+                ring_sem.at[slot, piece],
+            )
+            for piece in range(parts)
+        ]
+
+    bc_copy = pltpu.make_async_copy(bc_ref, bc_buf, bc_sem)
+    bc_copy.start()
+    for block in range(slots):
+        for copy in fetches(block, block):
+            copy.start()
+    source = lax.broadcasted_iota(jnp.int32, (128, 256), 0)
+    target = lax.broadcasted_iota(jnp.int32, (128, 256), 1)
+    spread = [(target == 2 * source + plane).astype(BF16) for plane in range(2)]
+    for piece in range(depth // 128):
+        part = x_ref[:, piece * 128 : (piece + 1) * 128]
+        for plane in range(2):
+            wide_x[plane * rows : (plane + 1) * rows, piece * 256 : (piece + 1) * 256] = jnp.dot(
+                part, spread[plane], preferred_element_type=F32
+            ).astype(BF16)
+    column = lax.broadcasted_iota(jnp.int32, (span, span), 0)
+    place = lax.broadcasted_iota(jnp.int32, (span, span), 1)
+    head = lax.shift_right_logical(column, shift_of(HEAD_DIM))
+    inner = lax.bitwise_and(column, HEAD_DIM - 1)
+    owner = lax.shift_right_logical(inner, shift_of(chan))
+    channel = lax.bitwise_and(inner, chan - 1)
+    order[...] = (place == owner * 128 + head * chan + channel).astype(BF16)
+
+    greet(("narrow",))
+    small_stage[...] = jnp.zeros_like(small_stage)
+    small_stage[:, bc_columns : bc_columns + dt_columns] = lax.dot_general(
+        x_ref[...], dt_ref[...], (((1,), (1,)), ((), ())), preferred_element_type=F32
+    ).astype(BF16)
+    bc_copy.wait()
+    small_stage[:, :bc_columns] = jnp.dot(
+        x_ref[...], bc_buf[...], preferred_element_type=F32
+    ).astype(BF16)
+
+    def small_copy(hop):
+        return pltpu.make_async_remote_copy(
+            src_ref=small_stage,
+            dst_ref=small_arrived.at[hop - 1],
+            send_sem=small_send.at[hop - 1],
+            recv_sem=small_recv.at[hop - 1],
+            device_id={"narrow": lax.rem(me + hop, parts)},
+            device_id_type=MESH,
+        )
+
+    def piece_copy(hop, block):
+        return pltpu.make_async_remote_copy(
+            src_ref=stage.at[lax.rem(me + hop, parts), block],
+            dst_ref=arrived.at[hop - 1, block],
+            send_sem=send_sem.at[hop - 1, block],
+            recv_sem=recv_sem.at[hop - 1, block],
+            device_id={"narrow": lax.rem(me + hop, parts)},
+            device_id_type=MESH,
+        )
+
+    for hop in range(1, parts):
+        small_copy(hop).start()
+
+    def step(block, carry):
+        slot = lax.rem(block, slots)
+        for copy in fetches(block, slot):
+            copy.wait()
+        weights = jnp.concatenate(
+            [ring[slot, piece].reshape(2 * depth, 128) for piece in range(parts)], axis=1
+        )
+        product = jnp.dot(wide_x[...], weights, preferred_element_type=F32).astype(BF16)
+
+        @pl.when(block + slots < blocks)
+        def _():
+            for copy in fetches(block + slots, slot):
+                copy.start()
+
+        sorted_out = jnp.dot(product, order[...], preferred_element_type=F32).astype(BF16)
+        for piece in range(parts):
+            stage[piece, block] = sorted_out[:, piece * 128 : (piece + 1) * 128]
+        for hop in range(1, parts):
+            piece_copy(hop, block).start()
+        return carry
+
+    lax.fori_loop(0, blocks, step, 0)
+    for hop in range(1, parts):
+        small_copy(hop).wait()
+    total = small_stage[...].astype(F32)
+    for hop in range(1, parts):
+        total = total + small_arrived[hop - 1].astype(F32)
+    small_ref[...] = total.astype(BF16)
+    for block in range(blocks):
+        total = stage[me, block].astype(F32)
+        for hop in range(1, parts):
+            piece_copy(hop, block).wait()
+            total = total + arrived[hop - 1, block].astype(F32)
+        mine_ref[:, block * 128 : (block + 1) * 128] = total.astype(BF16)
+
+
+def project(tok_rows, dt_weight, xz_weight, bc_weight):
+    parts = lax.axis_size("narrow")
+    rows, depth = tok_rows.shape
+    blocks = xz_weight.shape[2] // (128 * parts)
+    slots = min(3, blocks)
+    small = bc_weight.shape[1] + 128
+    vmem = pl.BlockSpec(memory_space=pltpu.VMEM)
+    anywhere = pl.BlockSpec(memory_space=pl.ANY)
+    return pl.pallas_call(
+        functools.partial(project_kernel, slots),
+        name="project",
+        out_shape=(
+            jax.ShapeDtypeStruct((2 * rows, 128 * blocks), BF16),
+            jax.ShapeDtypeStruct((rows, small), BF16),
+        ),
+        in_specs=[vmem, vmem, anywhere, anywhere],
+        out_specs=(vmem, vmem),
+        scratch_shapes=[
+            pltpu.VMEM((slots, parts, depth, 2, 128), BF16),
+            pltpu.VMEM(bc_weight.shape, BF16),
+            pltpu.VMEM((2 * rows, 2 * depth), BF16),
+            pltpu.VMEM((128 * parts, 128 * parts), BF16),
+            pltpu.VMEM((parts, blocks, 2 * rows, 128), BF16),
+            pltpu.VMEM((parts - 1, blocks, 2 * rows, 128), BF16),
+            pltpu.VMEM((rows, small), BF16),
+            pltpu.VMEM((parts - 1, rows, small), BF16),
+            pltpu.SemaphoreType.DMA((slots, parts)),
+            pltpu.SemaphoreType.DMA,
+            pltpu.SemaphoreType.DMA((parts - 1, blocks)),
+            pltpu.SemaphoreType.DMA((parts - 1, blocks)),
+            pltpu.SemaphoreType.DMA((parts - 1,)),
+            pltpu.SemaphoreType.DMA((parts - 1,)),
+        ],
+        compiler_params=pltpu.CompilerParams(
+            collective_id=0, has_side_effects=True, vmem_limit_bytes=VMEM_BYTES
+        ),
+    )(tok_rows, dt_weight.T, xz_weight, bc_weight)
+
+
+def finish_kernel(
+    groups_here,
+    gated_ref,
+    gain_ref,
+    w_ref,
+    out_ref,
+    w_buf,
+    squares,
+    squares_in,
+    normed,
+    total,
+    stage,
+    arrived,
+    w_sem,
+    sq_send,
+    sq_recv,
+    n_send,
+    n_recv,
+    o_send,
+    o_recv,
+):
+    wide = lax.axis_size("wide")
+    parts = lax.axis_size("narrow")
+    row = lax.axis_index("wide")
+    me = lax.axis_index("narrow")
+    rows, width = gated_ref.shape
+    columns = w_ref.shape[1] // parts
+
+    def fetch(hop):
+        first = pl.multiple_of(lax.rem(row - hop + wide, wide) * width, width)
+        return pltpu.make_async_copy(w_ref.at[pl.ds(first, width)], w_buf.at[hop], w_sem.at[hop])
+
+    def squares_copy(hop):
+        return pltpu.make_async_remote_copy(
+            src_ref=squares,
+            dst_ref=squares_in.at[hop - 1],
+            send_sem=sq_send.at[hop - 1],
+            recv_sem=sq_recv.at[hop - 1],
+            device_id={"narrow": lax.rem(me + hop, parts)},
+            device_id_type=MESH,
+        )
+
+    def normed_copy(hop):
+        return pltpu.make_async_remote_copy(
+            src_ref=normed.at[0],
+            dst_ref=normed.at[hop],
+            send_sem=n_send.at[hop - 1],
+            recv_sem=n_recv.at[hop - 1],
+            device_id={"wide": lax.rem(row + hop, wide)},
+            device_id_type=MESH,
+        )
+
+    def out_copy(hop):
+        return pltpu.make_async_remote_copy(
+            src_ref=stage.at[lax.rem(me + hop, parts)],
+            dst_ref=arrived.at[hop - 1],
+            send_sem=o_send.at[hop - 1],
+            recv_sem=o_recv.at[hop - 1],
+            device_id={"narrow": lax.rem(me + hop, parts)},
+            device_id_type=MESH,
+        )
+
+    for hop in range(wide):
+        fetch(hop).start()
+    greet(("narrow", "wide"))
+    gated = gated_ref[...]
+    if groups_here:
+        share = width // groups_here
+        lane = lax.broadcasted_iota(jnp.int32, (rows, 128), 1)
+        sums = jnp.zeros((rows, 128), F32)
+        for group in range(groups_here):
+            cut = gated[:, group * share : (group + 1) * share]
+            sums = jnp.where(lane == group, jnp.sum(cut * cut, axis=1, keepdims=True), sums)
+        squares[...] = sums
+        for hop in range(1, parts):
+            squares_copy(hop).start()
+        for hop in range(1, parts):
+            squares_copy(hop).wait()
+            sums = sums + squares_in[hop - 1]
+        inverse = lax.rsqrt(sums / (HEADS // NGROUPS * HEAD_DIM) + EPSILON)
+        for group in range(groups_here):
+            cut = slice(group * share, (group + 1) * share)
+            normed[0, :, cut] = (
+                gated[:, cut] * inverse[:, group : group + 1] * gain_ref[:, cut]
+            ).astype(BF16)
+    else:
+        normed[0] = (gated * gain_ref[...]).astype(BF16)
+    for hop in range(1, wide):
+        normed_copy(hop).start()
+    for hop in range(wide):
+        fetch(hop).wait()
+        if hop:
+            normed_copy(hop).wait()
+        part = jnp.dot(normed[hop], w_buf[hop], preferred_element_type=F32)
+        if hop:
+            part = part + total[...]
+        if hop < wide - 1:
+            total[...] = part
+        else:
+            for piece in range(parts):
+                stage[piece] = part[:, piece * columns : (piece + 1) * columns].astype(BF16)
+    for hop in range(1, parts):
+        out_copy(hop).start()
+    final = stage[me].astype(F32)
+    for hop in range(1, parts):
+        out_copy(hop).wait()
+        final = final + arrived[hop - 1].astype(F32)
+    out_ref[...] = final.astype(BF16)
+
+
+def finish(gated, gain, out_weight, groups_here):
+    parts = lax.axis_size("narrow")
+    wide = lax.axis_size("wide")
+    rows, width = gated.shape
+    columns = out_weight.shape[1] // parts
+    vmem = pl.BlockSpec(memory_space=pltpu.VMEM)
+    return pl.pallas_call(
+        functools.partial(finish_kernel, groups_here),
+        name="finish",
+        out_shape=jax.ShapeDtypeStruct((rows, columns), BF16),
+        in_specs=[vmem, vmem, pl.BlockSpec(memory_space=pl.ANY)],
+        out_specs=vmem,
+        scratch_shapes=[
+            pltpu.VMEM((wide, width, out_weight.shape[1]), BF16),
+            pltpu.VMEM((rows, 128), F32),
+            pltpu.VMEM((parts - 1, rows, 128), F32),
+            pltpu.VMEM((wide, rows, width), BF16),
+            pltpu.VMEM((rows, out_weight.shape[1]), F32),
+            pltpu.VMEM((parts, rows, columns), BF16),
+            pltpu.VMEM((parts - 1, rows, columns), BF16),
+            pltpu.SemaphoreType.DMA((wide,)),
+            pltpu.SemaphoreType.DMA((parts - 1,)),
+            pltpu.SemaphoreType.DMA((parts - 1,)),
+            pltpu.SemaphoreType.DMA((wide - 1,)),
+            pltpu.SemaphoreType.DMA((wide - 1,)),
+            pltpu.SemaphoreType.DMA((parts - 1,)),
+            pltpu.SemaphoreType.DMA((parts - 1,)),
+        ],
+        compiler_params=pltpu.CompilerParams(
+            collective_id=1, has_side_effects=True, vmem_limit_bytes=VMEM_BYTES
+        ),
+    )(gated, gain, out_weight)
 
 
 def shards(
@@ -74,22 +419,14 @@
     narrow_count = lax.axis_size("narrow")
     wide_index = lax.axis_index("wide")
     chan_local = HEAD_DIM // narrow_count
-    xz_local = xz_weight.reshape(xz_weight.shape[0], 2, head_local, HEAD_DIM)
-    bc_part = jnp.dot(tok_rows, bc_weight, preferred_element_type=jnp.float32)
-    dt_part = jnp.dot(tok_rows, dt_weight, preferred_element_type=jnp.float32)
-    xz_mine = lax.psum_scatter(
-        jnp.einsum("rd,dzhc->czrh", tok_rows, xz_local, preferred_element_type=jnp.float32),
-        "narrow",
-        scatter_dimension=0,
-        tiled=True,
-    )
-    bc_summed, dt_summed = lax.psum((bc_part, dt_part), "narrow")
-    xz_mine = xz_mine.astype(jnp.bfloat16)
-    xz_mine = jnp.transpose(xz_mine, (1, 2, 3, 0)).reshape(2, seq_count, 2, head_local, chan_local)
+    xz_mine, small = project(tok_rows, dt_weight, xz_weight, bc_weight)
+    bc_summed = small[:, : bc_weight.shape[1]]
+    dt_summed = small[:, bc_weight.shape[1] : bc_weight.shape[1] + head_local]
+    xz_mine = xz_mine.reshape(2, seq_count, 2, head_local, chan_local)
     gate_vals = xz_mine[0]
     x_proj = xz_mine[1]
-    bc_proj = bc_summed.astype(jnp.bfloat16).reshape(seq_count, 2, bc_summed.shape[1])
-    dt_proj = dt_summed.astype(jnp.bfloat16).reshape(seq_count, 2, head_local)
+    bc_proj = bc_summed.reshape(seq_count, 2, bc_summed.shape[1])
+    dt_proj = dt_summed.reshape(seq_count, 2, head_local)
     x_conv, new_conv_x = conv_tokens(conv_x_state, x_proj, conv_x_weight, conv_x_bias)
     bc_conv, new_conv_bc = conv_tokens(conv_bc_state, bc_proj, conv_bc_weight, conv_bc_bias)
     group_local = max(NGROUPS // wide_count, 1)
@@ -123,24 +460,18 @@
         readouts.append(readout)
     y_all = jnp.stack(readouts, axis=1)
     gated_out = y_all * jax.nn.silu(gate_vals.astype(jnp.float32))
-    grouped = gated_out.reshape(seq_count, 2, group_local, per_group * chan_local)
-    squares_part = jnp.sum(grouped * grouped, axis=-1)
-    group_sum = lax.psum(squares_part, "narrow")
-    for bit_idx in range(group_span.bit_length() - 1):
-        group_sum = group_sum + swapped(group_sum, "wide", bit_idx)
-    inverse = lax.rsqrt(group_sum / (HEADS // NGROUPS * HEAD_DIM) + EPSILON)
-    normed = (grouped * inverse[..., None]).reshape(
-        seq_count, 2, head_local, chan_local
-    ) * norm_weight.astype(jnp.float32)
-    normed = normed.astype(jnp.bfloat16).reshape(row_count, head_local, chan_local)
-    out_part = jnp.einsum(
-        "rhc,hcd->rd",
-        lax.all_gather(normed, "wide", axis=1, tiled=True),
-        out_weight,
-        preferred_element_type=jnp.float32,
-    )
-    out_mine = lax.psum_scatter(
-        out_part.astype(jnp.bfloat16), "narrow", scatter_dimension=1, tiled=True
+    gain = norm_weight.astype(jnp.float32).reshape(1, head_local * chan_local)
+    gated_rows = gated_out.reshape(row_count, head_local * chan_local)
+    if group_span > 1:
+        group_sum = lax.psum(jnp.sum(gated_rows * gated_rows, axis=1, keepdims=True), "narrow")
+        for bit_idx in range(group_span.bit_length() - 1):
+            group_sum = group_sum + swapped(group_sum, "wide", bit_idx)
+        gated_rows = gated_rows * lax.rsqrt(group_sum / (HEADS // NGROUPS * HEAD_DIM) + EPSILON)
+    out_mine = finish(
+        gated_rows,
+        gain,
+        out_weight.reshape(-1, out_weight.shape[2]),
+        group_local if group_span == 1 else 0,
     )
     layer_out = out_mine.reshape(seq_count, 2, out_mine.shape[1])
     return (layer_out, ssm_now, new_conv_x, new_conv_bc)

time: 254 us -> 107 us (0.42)
  local copies, waits for them, and re-layouts: 104 us -> 24.6 us
  Pallas kernels: 0 us -> 50.8 us
  blocking collectives: 43.9 us -> 0 us
  matrix products: 34.4 us -> 0 us
  waiting for transfers between devices: 22.5 us -> 0 us
  between operations: 14.6 us -> 1.02 us
    unnamed x52 -> x39, local copies, waits for them, and re-layouts: 87.9 us -> 5.49 us
    pallas_call x0 -> x2, Pallas kernels: none -> 50.8 us  [the longest x1 31 us: project(): pl.pallas_call(functools.partial(project_kernel, slots), name='project',...]
    dot_general x4 -> x0, matrix products: 34.4 us -> none  [the longest x1 21.7 us: shards(): jnp.einsum('rd,dzhc->czrh', tok_rows, xz_local, preferred_element_type=jn...]
    all_gather x1 -> x0, blocking collectives: 22.6 us -> none  [shards(): lax.all_gather(normed, 'wide', axis=1, tiled=True)]
    reduce_scatter x2 -> x0, waiting for transfers between devices: 22.5 us -> none  [the longest x1 17.4 us: shards(): lax.psum_scatter(out_part.astype(jnp.bfloat16), 'narrow', scatter_dimensi...]
    psum x2 -> x0, blocking collectives: 21.2 us -> none  [the longest x1 15.5 us: shards(): bc_summed, dt_summed = lax.psum((bc_part, dt_part), 'narrow')]
  transfers between devices with their start and end apart: 2 -> 0, of which waited for: 2 -> 0; matrix products, arithmetic and copies ran while one was open for 7% -> 0% of each run, Pallas kernels for 0% -> 0%
where the time goes in v1:
time: 107 us; the launch traced here: 106 us
  Pallas kernels  50.8 us (47%)
  other arithmetic  30 us (28%)
  local copies, waits for them, and re-layouts  24.6 us (23%)
    pallas_call x1, Pallas kernels, project(): pl.pallas_call(functools.partial(project_kernel, slots), name='project',...  31 us
    reduce_sum x1, other arithmetic, advance(): jnp.sum(ssm_now * c_tok[:, :, None, :], axis=-1)  21.8 us
    pallas_call x1, Pallas kernels, finish(): pl.pallas_call(functools.partial(finish_kernel, groups_here), name='finis...  19.9 us
    unnamed x39, local copies, waits for them, and re-layouts  5.49 us
    mul x4, local copies, waits for them, and re-layouts, conv_tokens(): tap_weights[tap_idx].astype(jnp.float32)  4.93 us
    concatenate x2, other arithmetic, conv_tokens(): window = jnp.concatenate([history, fresh_vals], axis=1)  2.33 us

profile of v1, /device:TPU:0, one launch (start us, length us, event | category | flops | bytes accessed | tf_op | source)
XLA Modules:
  0.0 106.4 jit_solution(13057550770713707387)
XLA Ops:
  0.6 1.6 %reshape.309.x_ref = bf16[40,2048]{1,0:T(8,128)(2,1)} reshape(bf16[20,2,2048]{2,1,0:T(2,128)(2,1)} %param.16) | data formatting | bytes 327680 | tf_op jit(solution)/shard_map/reshape | solution.py:416
  2.3 31.0 %project.1 = (bf16[80,1024]{1,0:T(8,128)(2,1)}, bf16[40,1152]{1,0:T(8,128)(2,1)}) custom-call(bf16[40,2048]{1,0:T(8,128)(2,1)} %reshape.309.x_ref, bf16[64,2048]{1,0:T(8,128)(2,1)} %bitcast.129, bf16[2048,2,4096]{2,1,0:T(2,128)(2,1)} %w_ref.1, bf16[2048,1024]{1,0:T(8,128)(2,1)} %bc_ref.1), custom_call_target="tpu_custom_call" | custom-call | tf_op jit(solution)/shard_map/project/pallas_call | solution.py:221
  33.2 0.0 copy-start.16
  33.3 0.0 copy-start.14
  33.3 0.0 copy-start.12
  33.3 0.0 copy-start.3
  33.3 0.9 slice.130
  34.4 0.1 divide_multiply_fusion
  34.5 0.1 stack.16
  34.6 0.1 stack.17
  34.7 0.1 fusion.42
  34.8 0.1 copy_bitcast_fusion
  34.9 0.2 broadcast_in_dim.5
  35.1 0.3 slice_bitcast_fusion.2
  35.4 0.2 broadcast_in_dim.4
  35.7 1.8 %slice_bitcast_fusion.3 = (f32[20,64,256]{2,1,0:T(8,128)}, f32[20,64,256]{2,1,0:T(8,128)}) fusion(f32[20,2,64,256]{3,2,0,1:T(8,128)S(1)} %bitcast.128), kind=kLoop, calls=%fused_computation.7 | loop fusion | bytes 5242880 | tf_op jit(solution)/shard_map/mul | solution.py:49
  37.5 0.7 slice.112
  38.2 0.6 multiply_exponential_fusion
  38.8 0.0 copy-done.10
  38.9 0.6 slice.121
  39.5 1.4 %squeeze.6 = bf16[20,2,64,16]{3,2,1,0:T(8,128)(2,1)S(1)} reshape(bf16[40,1024]{1,0:T(8,128)(2,1)} %slice.121) | data formatting | bytes 163840 | tf_op jit(solution)/shard_map/squeeze | solution.py:427
  40.9 0.6 bitcast_convert_fusion.3
  41.5 0.8 copy.80
  42.3 1.4 %copy.82 = f32[64,16]{1,0:T(8,128)} copy(f32[64,16]{0,1:T(8,128)} %get-tuple-element.27) | data formatting | bytes 8192 | tf_op jit(solution)/shard_map/mul | solution.py:39
  43.6 1.4 %copy.84 = f32[64,16]{1,0:T(8,128)} copy(f32[64,16]{0,1:T(8,128)} %get-tuple-element.29) | data formatting | bytes 8192 | tf_op jit(solution)/shard_map/mul | solution.py:39
  45.0 1.4 %copy.86 = f32[64,16]{1,0:T(8,128)} copy(f32[64,16]{0,1:T(8,128)} %get-tuple-element.28) | data formatting | bytes 8192 | tf_op jit(solution)/shard_map/mul | solution.py:39
  46.4 0.7 fusion.41
  47.1 1.8 %copy.101 = bf16[20,1,64,16]{3,2,1,0:T(8,128)(2,1)} copy(bf16[20,1,64,16]{2,3,1,0:T(8,128)(2,1)} %get-tuple-element.21) | data formatting | bytes 81920
  48.9 1.8 %copy.102 = bf16[20,1,64,16]{3,2,1,0:T(8,128)(2,1)} copy(bf16[20,1,64,16]{2,3,1,0:T(8,128)(2,1)} %get-tuple-element.22) | data formatting | bytes 81920
  50.6 1.8 %copy.103 = bf16[20,1,64,16]{3,2,1,0:T(8,128)(2,1)} copy(bf16[20,1,64,16]{2,3,1,0:T(8,128)(2,1)} %get-tuple-element.23) | data formatting | bytes 81920
  52.4 1.4 %copy.79 = f32[64,16]{1,0:T(8,128)} copy(bf16[64,16]{0,1:T(8,128)(2,1)} %param.21) | data formatting | bytes 6144 | tf_op jit(solution)/shard_map/convert_element_type | solution.py:37
  53.8 2.0 %multiply_multiply_fusion.1 = (f32[20,64,16]{2,1,0:T(8,128)S(1)}, f32[20,64,16]{2,1,0:T(8,128)S(1)}) fusion(bf16[20,1,64,16]{3,2,1,0:T(8,128)(2,1)} %copy.103, bf16[20,1,64,16]{3,2,1,0:T(8,128)(2,1)} %copy.102, bf16[20,1,64,16]{3,2,1,0:T(8,128)(2,1)} %copy.101, f32[64,16]{1,0:T(8,128)} %copy.86, f32[64,16]{1,0:T(8,128)} %copy.84, f32[64,16]{1,0:T(8,128)} %copy.82, ...), kind=kLoop, calls=%fused_computation.49 | loop fusion | flops 634880 | bytes 399360 | tf_op jit(solution)/shard_map/mul | solution.py:49
  55.8 0.0 copy-start.8
  55.8 0.0 copy-start.9
  55.8 0.0 copy-start.15
  55.9 21.8 %multiply_reduce_fusion = (f32[20,64,16]{2,1,0:T(8,128)S(1)}, f32[20,64,16,256]{3,2,1,0:T(8,128)}, f32[20,64,16]{2,1,0:T(8,128)S(1)}) fusion(f32[20,64,256]{2,1,0:T(8,128)S(1)} %get-tuple-element.12, f32[20,64,256]{2,1,0:T(8,128)} %get-tuple-element.14, f32[20,64,16]{2,1,0:T(8,128)S(1)} %get-tuple-element.18, f32[20,64,256]{2,1,0:T(8,128)} %get-tuple-element.13, ...), kind=kLoop, calls=%fused_computation | loop fusion | flops 52387840 | bytes 47523840 | tf_op jit(solution)/shard_map/reduce_sum | solution.py:51
  77.6 0.0 copy-done
  77.7 0.8 bitcast_add_fusion.1
  78.5 0.2 pad_maximum_fusion
  78.7 0.8 stack.20
  79.5 1.6 %fusion.27.gated_ref = f32[40,1024]{1,0:T(8,128)} fusion(f32[40,1024]{1,0:T(8,128)S(1)} %stack.20, bf16[80,1024]{1,0:T(8,128)(2,1)} %get-tuple-element.7), kind=kLoop, calls=%fused_computation.56 | loop fusion | flops 245760 | bytes 409600 | tf_op jit(solution)/shard_map/mul | solution.py:462
  81.1 0.8 copy.94
  81.9 0.7 reshape.334.gain_ref
  82.5 19.9 %finish.1 = bf16[40,512]{1,0:T(8,128)(2,1)} custom-call(f32[40,1024]{1,0:T(8,128)} %fusion.27.gated_ref, f32[1,1024]{1,0:T(1,128)} %reshape.334.gain_ref, bf16[4096,2048]{1,0:T(8,128)(2,1)} %bitcast.126), custom_call_target="tpu_custom_call" | custom-call | tf_op jit(solution)/shard_map/finish/pallas_call | solution.py:368
  102.4 1.4 %reshape.317 = bf16[20,2,512]{2,1,0:T(2,128)(2,1)} reshape(bf16[40,512]{1,0:T(8,128)(2,1)} %finish.1) | data formatting | bytes 81920 | tf_op jit(solution)/shard_map/reshape | solution.py:476
  103.8 0.2 copy.95
  104.1 0.8 pad_maximum_fusion.1
  104.8 1.6 %pad_maximum_fusion.2 = bf16[20,3,1024]{2,0,1:T(8,128)(2,1)} fusion(bf16[20,2,1024]{2,0,1:T(8,128)(2,1)} %copy-done.4, bf16[20,3,1024]{2,0,1:T(8,128)(2,1)} %param.25), kind=kLoop, calls=%fused_computation.57 | loop fusion | flops 61440 | bytes 327680 | tf_op jit(solution)/shard_map/concatenate | solution.py:34
  (33 shorter events, 0.2 us)
Async XLA Ops:
  2.3 32.0 %copy-start.11 = (bf16[4,1024]{1,0:T(4,128)(2,1)S(1)}, bf16[4,1024]{1,0:T(4,128)(2,1)}, u32[]{:S(2)}) copy-start(bf16[4,1024]{1,0:T(4,128)(2,1)} %param.22) | copy-start | bytes 24580
  2.3 32.1 %copy-start.13 = (bf16[1024]{0:T(1024)(128)(2,1)S(1)}, bf16[1024]{0:T(1024)(128)(2,1)}, u32[]{:S(2)}) copy-start(bf16[1024]{0:T(1024)(128)(2,1)} %param.23) | copy-start | bytes 6148
  2.3 32.1 %copy-start.5 = (bf16[20,3,1024]{2,0,1:T(8,128)(2,1)S(1)}, bf16[20,3,1024]{2,0,1:T(8,128)(2,1)}, u32[]{:S(2)}) copy-start(bf16[20,3,1024]{2,0,1:T(8,128)(2,1)} %param.25) | copy-start | bytes 368644
  33.2 4.9 %copy-start.16 = (f32[64]{0:T(128)S(1)}, f32[64]{0:T(128)}, u32[]{:S(2)}) copy-start(f32[64]{0:T(128)} %param.27) | copy-start | bytes 772
  33.3 4.9 %copy-start.14 = (f32[64]{0:T(128)S(1)}, f32[64]{0:T(128)}, u32[]{:S(2)}) copy-start(f32[64]{0:T(128)} %param.26) | copy-start | bytes 772
  33.3 7.6 %copy-start.12 = (bf16[4,64,16]{1,2,0:T(8,128)(2,1)S(1)}, bf16[4,64,16]{1,2,0:T(8,128)(2,1)}, u32[]{:S(2)}) copy-start(bf16[4,64,16]{1,2,0:T(8,128)(2,1)} %param.20) | copy-start | bytes 24580
  33.3 13.1 %copy-start.3 = (bf16[20,3,64,16]{2,3,1,0:T(8,128)(2,1)S(1)}, bf16[20,3,64,16]{2,3,1,0:T(8,128)(2,1)}, u32[]{:S(2)}) copy-start(bf16[20,3,64,16]{2,3,1,0:T(8,128)(2,1)} %param.24) | copy-start | bytes 368644
  34.3 0.8 copy-start.4
  34.7 4.2 %copy-start.10 = (bf16[80,1024]{1,0:T(8,128)(2,1)S(1)}, bf16[80,1024]{1,0:T(8,128)(2,1)}, u32[]{:S(2)}) copy-start(bf16[80,1024]{1,0:T(8,128)(2,1)} %get-tuple-element.7) | copy-start | bytes 491524
  55.8 21.9 %copy-start = (bf16[20,1,64,16]{3,2,1,0:T(8,128)(2,1)S(1)}, bf16[20,1,64,16]{3,2,1,0:T(8,128)(2,1)}, u32[]{:S(2)}) copy-start(bf16[20,1,64,16]{3,2,1,0:T(8,128)(2,1)} %copy.101) | copy-start | bytes 122884
  55.8 21.9 %copy-start.1 = (bf16[20,1,64,16]{3,2,1,0:T(8,128)(2,1)S(1)}, bf16[20,1,64,16]{3,2,1,0:T(8,128)(2,1)}, u32[]{:S(2)}) copy-start(bf16[20,1,64,16]{3,2,1,0:T(8,128)(2,1)} %copy.102) | copy-start | bytes 122884
  55.8 21.9 %copy-start.2 = (bf16[20,1,64,16]{3,2,1,0:T(8,128)(2,1)S(1)}, bf16[20,1,64,16]{3,2,1,0:T(8,128)(2,1)}, u32[]{:S(2)}) copy-start(bf16[20,1,64,16]{3,2,1,0:T(8,128)(2,1)} %copy.103) | copy-start | bytes 122884
  55.8 21.9 %copy-start.6 = (f32[64,16]{1,0:T(8,128)S(1)}, f32[64,16]{1,0:T(8,128)}, u32[]{:S(2)}) copy-start(f32[64,16]{1,0:T(8,128)} %copy.82) | copy-start | bytes 12292
  55.8 21.9 %copy-start.7 = (f32[64,16]{1,0:T(8,128)S(1)}, f32[64,16]{1,0:T(8,128)}, u32[]{:S(2)}) copy-start(f32[64,16]{1,0:T(8,128)} %copy.84) | copy-start | bytes 12292
  55.8 21.9 %copy-start.8 = (f32[64,16]{1,0:T(8,128)S(1)}, f32[64,16]{1,0:T(8,128)}, u32[]{:S(2)}) copy-start(f32[64,16]{1,0:T(8,128)} %copy.86) | copy-start | bytes 12292
  55.8 21.9 %copy-start.9 = (f32[64,16]{1,0:T(8,128)S(1)}, f32[64,16]{1,0:T(8,128)}, u32[]{:S(2)}) copy-start(f32[64,16]{1,0:T(8,128)} %copy.79) | copy-start | bytes 12292
  55.8 21.9 %copy-start.15 = (f32[64]{0:T(128)S(1)}, f32[64]{0:T(128)}, u32[]{:S(2)}) copy-start(f32[64]{0:T(128)} %param.28) | copy-start | bytes 772
